TPU v7x, 32 devices: a whole 2x2x4 slice. The times are simulated.
32 devices in a mesh: dp: 16 (over z, y, x), section: 2 (over core).
Axes of the slice: x: 2, y: 2, z: 4, core: 2. Of those that a mesh axis runs over, the one named last changes fastest.
Arguments:
- section_inputs: bfloat16 [2, 2, 2048, 2048], P('section', None, 'dp'), may hold values from -6 to 6
- mix_weight: bfloat16 [2, 2048, 2048], P('section'), may hold values from -0.0625 to 0.0625
- norm_gain: float32 [2, 2048], P('section'), may hold values from 0.5 to 1.5
- out_cotangent: bfloat16 [2, 2048, 2048], P(None, 'dp'), may hold values from -6 to 6
- positions: int32 [2, 2048], P(None, 'dp'), may hold values from 0 to 1023
Outputs:
- grad_inputs: bfloat16 [2, 2, 2048, 2048], P('section', None, 'dp')
- grad_weight: float32 [2, 2048, 2048], P('section', 'dp')
- grad_gain: float32 [2, 2048], P('section', 'dp')
Inputs may be any that keep to these rules, and one draw needn't show every extreme that they name: `positions`: depth index of a token within its tile.
All inputs are finite; a program needn't handle non-finite values.
Results may differ from a plain program's by a relative error of at most 0.017.
Values may be sent and summed in bfloat16 or wider, within the bound.
A program may use at most 128 MiB of HBM per device.

v0:
```python
import math

import jax
import jax.numpy as jnp
from jax import lax
from jax.sharding import PartitionSpec as P

DEPTH = 1024


def from_behind(shard, axis, by):
    peers = lax.axis_size(axis)
    pairs = [(i, i + by) for i in range(peers) if 0 <= i + by < peers]
    return lax.ppermute(shard, axis, pairs)


def section_back(inputs, grad_out, factor, gain_vec, weight_mat):
    inputs_f = inputs.astype(jnp.float32)
    inv_rms = lax.rsqrt(jnp.mean(inputs_f * inputs_f, axis=-1, keepdims=True) + 1e-06)
    normed = inputs_f * inv_rms * gain_vec
    activation, gelu_back = jax.vjp(jax.nn.gelu, normed)
    upstream = (factor[:, None] * grad_out.astype(jnp.float32)).astype(jnp.bfloat16)
    back = lax.dot_general(
        upstream, weight_mat, (((1,), (1,)), ((), ())), preferred_element_type=jnp.float32
    )
    grad_norm = gelu_back(back)[0]
    scaled = grad_norm * gain_vec
    projected = jnp.mean(scaled * inputs_f, axis=-1, keepdims=True)
    delta = inv_rms * scaled - inputs_f * (inv_rms * inv_rms * inv_rms) * projected
    grad_in = (grad_out.astype(jnp.float32) + delta).astype(jnp.bfloat16)
    gain_term = jnp.sum(grad_norm * inputs_f * inv_rms, axis=0)
    return (grad_in, upstream, activation.astype(jnp.bfloat16), gain_term)


def body(section_inputs, mix_weight, norm_gain, out_cotangent, positions):
    section_count = lax.axis_size("section")
    section_id = lax.axis_index("section")
    micro_count = section_inputs.shape[1]
    tok_mb = section_inputs.shape[2]
    channels = section_inputs.shape[3]
    total_rows = micro_count * tok_mb
    flat_inputs = section_inputs[0].reshape(total_rows, channels)
    flat_cot = out_cotangent.reshape(total_rows, channels)
    depth_gain = 1.0 + 0.5 * jnp.sin(
        2.0 * math.pi * positions.reshape(total_rows).astype(jnp.float32) / DEPTH
    )
    weight_mat = mix_weight[0]
    gain_vec = norm_gain[0]
    piece_count = 1
    unit_rows = tok_mb // piece_count
    unit_count = micro_count * piece_count
    tick_count = unit_count + section_count - 1

    def tick(step_idx, state_tuple):
        received, grads, saved_up, saved_act, gain_grad = state_tuple
        unit = step_idx - (section_count - 1 - section_id)
        active = jnp.logical_and(unit >= 0, unit < unit_count)
        offset = jnp.clip(unit, 0, unit_count - 1) * unit_rows
        inputs = lax.dynamic_slice_in_dim(flat_inputs, offset, unit_rows, 0)
        cot_rows = lax.dynamic_slice_in_dim(flat_cot, offset, unit_rows, 0)
        factor = lax.dynamic_slice_in_dim(depth_gain, offset, unit_rows, 0)
        grad_out = jnp.where(section_id == section_count - 1, cot_rows, received)
        grad_in, upstream, activation, gain_term = section_back(
            inputs, grad_out, factor, gain_vec, weight_mat
        )
        old_grad = lax.dynamic_slice_in_dim(grads, offset, unit_rows, 0)
        grads = lax.dynamic_update_slice_in_dim(
            grads, jnp.where(active, grad_in, old_grad), offset, 0
        )
        old_up = lax.dynamic_slice_in_dim(saved_up, offset, unit_rows, 0)
        saved_up = lax.dynamic_update_slice_in_dim(
            saved_up, jnp.where(active, upstream, old_up), offset, 0
        )
        old_act = lax.dynamic_slice_in_dim(saved_act, offset, unit_rows, 0)
        saved_act = lax.dynamic_update_slice_in_dim(
            saved_act, jnp.where(active, activation, old_act), offset, 0
        )
        gain_grad = gain_grad + jnp.where(active, gain_term, jnp.zeros_like(gain_term))
        received = from_behind(grad_in, "section", -1)
        return (received, grads, saved_up, saved_act, gain_grad)

    start_state = (
        jnp.zeros((unit_rows, channels), jnp.bfloat16),
        jnp.zeros((total_rows, channels), jnp.bfloat16),
        jnp.zeros((total_rows, channels), jnp.bfloat16),
        jnp.zeros((total_rows, channels), jnp.bfloat16),
        jnp.zeros((channels,), jnp.float32),
    )
    share_rows = channels // lax.axis_size("dp")
    state = lax.fori_loop(0, tick_count, tick, start_state)
    received, grads, saved_up, saved_act, gain_grad = state
    blocks = []
    for micro in range(0, 0 + micro_count):
        row_start = micro * tok_mb
        up_rows = lax.slice_in_dim(saved_up, row_start, row_start + tok_mb, axis=0)
        rows = lax.slice_in_dim(saved_act, row_start, row_start + tok_mb, axis=0)
        blocks.append(
            lax.dot_general(
                rows, up_rows, (((0,), (0,)), ((), ())), preferred_element_type=jnp.float32
            )
        )
    summed = lax.psum_scatter(
        jnp.concatenate(blocks, axis=1).astype(jnp.bfloat16), "dp", scatter_dimension=0, tiled=True
    ).astype(jnp.float32)
    weight_grad = jnp.sum(summed.reshape(share_rows, micro_count, channels), axis=1)
    gain_share = lax.psum_scatter(gain_grad, "dp", scatter_dimension=0, tiled=True)
    return (grads.reshape(1, micro_count, tok_mb, channels), weight_grad[None], gain_share[None])


def solution(mesh):
    return jax.shard_map(
        body,
        mesh=mesh,
        in_specs=(
            P("section", None, "dp", None),
            P("section", None, None),
            P("section", None),
            P(None, "dp", None),
            P(None, "dp"),
        ),
        out_specs=(P("section", None, "dp", None), P("section", "dp", None), P("section", "dp")),
        check_vma=False,
    )
```

profile of v0, /device:TPU:0, one launch (start us, length us, event | category | flops | bytes accessed | tf_op | source)
XLA Modules:
  0.0 455.2 jit_solution(7558354383748431101)
XLA Ops:
  9.3 51.3 %while.24 = (s32[]{:T(128)}, bf16[128,2048]{1,0:T(8,128)(2,1)S(1)}, bf16[256,2048]{1,0:T(8,128)(2,1)}, bf16[256,2048]{1,0:T(8,128)(2,1)S(1)}, bf16[256,2048]{1,0...) while((s32[]{:T(128)}, bf16[128,2048]{1,0:T(8,128)(2,1)S(1)}, ...), condition=%wide.region_4.5_spmd.clone, body=%wide.region_0.4_spmd.clone.sunk | while | flops 1089737088 | bytes 33120204 | solution.py:90
  10.7 1.4 select_dynamic-update-slice_fusion.4
  12.1 7.3 %fusion.37 = (f32[2048]{0:T(1024)S(1)}, f32[128]{0:T(128)S(1)}, f32[128,2048]{1,0:T(8,128)S(1)}) fusion(f32[128]{0:T(128)S(1)} %get-tuple-element.473, bf16[256,2048]{1,0:T(8,128)(2,1)} %get-tuple-element.528, s32[]{:T(128)S(6)} %select_n.140, f32[2048]{0:T(1024)} %bitcast.24, bf16[2048,2048]{1,0:T(8,128)(2,1)} %get-tuple-element.530, ...), kind=kOutput, calls=%fused_computation.28.clone.1 | convolution fusion | flops 1081866112 | bytes 10503684 | tf_op jit(solution)/shard_map/while/body/eval_jaxpr/dot_general | solution.py:23
  19.4 2.0 select_dynamic-update-slice_fusion.5
  22.4 1.3 collective-permute-start
  23.7 2.7 collective-permute-done
  27.8 1.4 select_dynamic-update-slice_fusion.4
  29.2 7.3 %fusion.37 = (f32[2048]{0:T(1024)S(1)}, f32[128]{0:T(128)S(1)}, f32[128,2048]{1,0:T(8,128)S(1)}) fusion(f32[128]{0:T(128)S(1)} %get-tuple-element.473, bf16[256,2048]{1,0:T(8,128)(2,1)} %get-tuple-element.528, s32[]{:T(128)S(6)} %select_n.140, f32[2048]{0:T(1024)} %bitcast.24, bf16[2048,2048]{1,0:T(8,128)(2,1)} %get-tuple-element.530, ...), kind=kOutput, calls=%fused_computation.28.clone.1 | convolution fusion | flops 1081866112 | bytes 10503684 | tf_op jit(solution)/shard_map/while/body/eval_jaxpr/dot_general | solution.py:23
  36.5 2.0 select_dynamic-update-slice_fusion.5
  39.5 1.3 collective-permute-start
  40.8 2.7 collective-permute-done
  44.9 1.4 select_dynamic-update-slice_fusion.4
  46.3 7.3 %fusion.37 = (f32[2048]{0:T(1024)S(1)}, f32[128]{0:T(128)S(1)}, f32[128,2048]{1,0:T(8,128)S(1)}) fusion(f32[128]{0:T(128)S(1)} %get-tuple-element.473, bf16[256,2048]{1,0:T(8,128)(2,1)} %get-tuple-element.528, s32[]{:T(128)S(6)} %select_n.140, f32[2048]{0:T(1024)} %bitcast.24, bf16[2048,2048]{1,0:T(8,128)(2,1)} %get-tuple-element.530, ...), kind=kOutput, calls=%fused_computation.28.clone.1 | convolution fusion | flops 1081866112 | bytes 10503684 | tf_op jit(solution)/shard_map/while/body/eval_jaxpr/dot_general | solution.py:23
  53.6 2.0 select_dynamic-update-slice_fusion.5
  56.6 1.3 collective-permute-start
  58.0 2.7 collective-permute-done
  60.6 2.4 convolution_convert_fusion.1
  63.0 2.4 convolution_convert_fusion
  65.4 7.5 %pad_maximum_fusion = bf16[2048,4096]{0,1:T(8,128)(2,1)} fusion(bf16[2048,2048]{0,1:T(8,128)(2,1)S(1)} %convolution_convert_fusion, bf16[2048,2048]{0,1:T(8,128)(2,1)S(1)} %convolution_convert_fusion.1), kind=kLoop, calls=%fused_computation.39 | loop fusion | flops 33554432 | bytes 33554432 | tf_op jit(solution)/shard_map/concatenate | solution.py:103
  72.9 20.7 %copy.9 = bf16[2048,4096]{1,0:T(8,128)(2,1)} copy(bf16[2048,4096]{0,1:T(8,128)(2,1)} %pad_maximum_fusion) | data formatting | bytes 33554432
  95.5 57.9 %all-reduce = f32[2048]{0:T(1024)S(1)} all-reduce(f32[2048]{0:T(1024)S(1)} %get-tuple-element.302), channel_id=3, replica_groups=mesh['dp'=16,'section'=2] {'dp'}, use_global_device_ids=true, to_apply=%region_7.8.clone | all-reduce | flops 2048 | bytes 16384
  154.0 291.2 %reduce-scatter.4.cloned.1.call-done = bf16[128,4096]{1,0:T(8,128)(2,1)} async-done(((bf16[2048,4096]{1,0:T(8,128)(2,1)}), bf16[128,4096]{1,0:T(8,128)(2,1)}) %reduce-scatter.4.cloned.1.call-update) | async-done | bytes 1048592
  445.2 1.6 copy.10
  447.0 1.3 copy.8
  (52 shorter events, 11.0 us)
Async XLA Ops:
  7.2 438.1 %reduce-scatter.4.cloned.1.call-start = ((), (), s32[]{:S(2)}) async-start(), calls=%async_computation.1 | async-start | bytes 17825792
  12.1 7.3 %copy-start = (bf16[256,2048]{1,0:T(8,128)(2,1)S(1)}, bf16[256,2048]{1,0:T(8,128)(2,1)}, u32[]{:S(2)}) copy-start(bf16[256,2048]{1,0:T(8,128)(2,1)} %get-tuple-element.528) | copy-start | bytes 3145732 | tf_op jit(solution)/shard_map/while
  12.1 7.3 %copy-start.1 = (bf16[256,2048]{1,0:T(8,128)(2,1)S(1)}, bf16[256,2048]{1,0:T(8,128)(2,1)}, u32[]{:S(2)}) copy-start(bf16[256,2048]{1,0:T(8,128)(2,1)} %get-tuple-element.503) | copy-start | bytes 3145732 | tf_op jit(solution)/shard_map/while
  12.1 7.3 %copy-start.3 = (f32[1,2048]{1,0:T(1,128)S(1)}, f32[1,2048]{1,0:T(1,128)}, u32[]{:S(2)}) copy-start(f32[1,2048]{1,0:T(1,128)} %get-tuple-element.531) | copy-start | bytes 24580 | tf_op jit(solution)/shard_map/while
  21.5 1.0 copy-start.2
  22.4 4.0 collective-permute-start
  29.2 7.3 %copy-start = (bf16[256,2048]{1,0:T(8,128)(2,1)S(1)}, bf16[256,2048]{1,0:T(8,128)(2,1)}, u32[]{:S(2)}) copy-start(bf16[256,2048]{1,0:T(8,128)(2,1)} %get-tuple-element.528) | copy-start | bytes 3145732 | tf_op jit(solution)/shard_map/while
  29.2 7.3 %copy-start.1 = (bf16[256,2048]{1,0:T(8,128)(2,1)S(1)}, bf16[256,2048]{1,0:T(8,128)(2,1)}, u32[]{:S(2)}) copy-start(bf16[256,2048]{1,0:T(8,128)(2,1)} %get-tuple-element.503) | copy-start | bytes 3145732 | tf_op jit(solution)/shard_map/while
  29.2 7.3 %copy-start.3 = (f32[1,2048]{1,0:T(1,128)S(1)}, f32[1,2048]{1,0:T(1,128)}, u32[]{:S(2)}) copy-start(f32[1,2048]{1,0:T(1,128)} %get-tuple-element.531) | copy-start | bytes 24580 | tf_op jit(solution)/shard_map/while
  38.6 1.0 copy-start.2
  39.5 4.0 collective-permute-start
  46.3 7.3 %copy-start = (bf16[256,2048]{1,0:T(8,128)(2,1)S(1)}, bf16[256,2048]{1,0:T(8,128)(2,1)}, u32[]{:S(2)}) copy-start(bf16[256,2048]{1,0:T(8,128)(2,1)} %get-tuple-element.528) | copy-start | bytes 3145732 | tf_op jit(solution)/shard_map/while
  46.3 7.3 %copy-start.1 = (bf16[256,2048]{1,0:T(8,128)(2,1)S(1)}, bf16[256,2048]{1,0:T(8,128)(2,1)}, u32[]{:S(2)}) copy-start(bf16[256,2048]{1,0:T(8,128)(2,1)} %get-tuple-element.503) | copy-start | bytes 3145732 | tf_op jit(solution)/shard_map/while
  46.3 7.3 %copy-start.3 = (f32[1,2048]{1,0:T(1,128)S(1)}, f32[1,2048]{1,0:T(1,128)}, u32[]{:S(2)}) copy-start(f32[1,2048]{1,0:T(1,128)} %get-tuple-element.531) | copy-start | bytes 24580 | tf_op jit(solution)/shard_map/while
  55.7 1.0 copy-start.2
  56.6 4.0 collective-permute-start
  93.6 0.7 copy-start.4
Sparse Core Ops, SparseCore 0:
  93.8 351.4 reduce-scatter.3
where the time goes:
time: 460 us; the launch traced here: 455 us
  waiting for transfers between devices  299 us (65%)
  blocking collectives  57.9 us (13%)
  local copies, waits for them, and re-layouts  30 us (7%)
  matrix products  26.6 us (6%)
  other arithmetic  22.5 us (5%)
  between operations  14.8 us (3%)
    unnamed x2, waiting for transfers between devices  291 us
    unnamed x1, blocking collectives  57.9 us
    unnamed x6, local copies, waits for them, and re-layouts  24.9 us
    dot_general x3, matrix products, section_back(): lax.dot_general(upstream, weight_mat, (((1,), (1,)), ((), ())), preferred...  21.9 us
  transfers between devices with their start and end apart: 4, of which 4 were waited for; matrix products, arithmetic and copies ran while one was open for 0% of the time, Pallas kernels for 0%

commit v1 on v0

v1 whole, which is shorter than its diff:
```python
import functools
import math

import jax
import jax.numpy as jnp
from jax import lax
from jax.experimental import pallas as pl
from jax.experimental.pallas import tpu as pltpu
from jax.sharding import PartitionSpec as P

DEPTH = 1024
MESH = pl.DeviceIdType.MESH
F32 = jnp.float32
BF16 = jnp.bfloat16


def outer_sum(a, b):
    return lax.dot_general(a, b, (((0,), (0,)), ((), ())), preferred_element_type=F32)


def weight_kernel(
    planes, act_ref, up_ref, gain_ref, out_ref, gain_out,
    gath_a, gath_u, part, from_left, from_right, to_right, to_left, swap_out, swap_in,
    gain_in, gain_mid, gain_sum, gain_z,
    xy_send, xy_recv, r_send, r_recv, l_send, l_recv, g_send, g_recv,
):
    me = lax.axis_index("dp")
    total = planes * 4
    x = lax.rem(me, 2)
    y = lax.rem(me // 2, 2)
    z = me // 4
    xn = me + 1 - 2 * x
    yn = me + 2 - 4 * y
    half = act_ref.shape[2]
    rows = half // planes
    share = rows // 2

    def copy(src, dst, send, recv, to):
        return pltpu.make_async_remote_copy(
            src_ref=src, dst_ref=dst, send_sem=send, recv_sem=recv,
            device_id={"dp": to}, device_id_type=MESH,
        )

    barrier = pltpu.get_barrier_semaphore()
    z_peers = [lax.rem(me + 4 * step, total) for step in range(1, planes)]
    for peer in [xn, yn] + z_peers:
        pl.semaphore_signal(barrier, inc=1, device_id={"dp": peer}, device_id_type=MESH)
    pl.semaphore_wait(barrier, 1 + planes)

    gain_x = copy(gain_ref, gain_in.at[0], g_send.at[0], g_recv.at[0], xn)
    act_x = copy(act_ref.at[1 - x], gath_a.at[0], xy_send.at[0], xy_recv.at[0], xn)
    up_y = copy(up_ref.at[1 - y], gath_u.at[1], xy_send.at[1], xy_recv.at[1], yn)
    up_x = copy(up_ref.at[y], gath_u.at[0], xy_send.at[2], xy_recv.at[2], xn)
    act_y = copy(act_ref.at[x], gath_a.at[1], xy_send.at[3], xy_recv.at[3], yn)
    act_d = copy(gath_a.at[0], gath_a.at[2], xy_send.at[4], xy_recv.at[4], yn)
    up_d = copy(gath_u.at[1], gath_u.at[2], xy_send.at[5], xy_recv.at[5], xn)
    gain_y = copy(gain_mid, gain_in.at[1], g_send.at[1], g_recv.at[1], yn)

    for first in (gain_x, act_x, up_y, up_x, act_y):
        first.start()

    @pl.loop(0, planes)
    def _(b):
        cols = pl.ds(pl.multiple_of(b * rows, 128), rows)
        part[b] = outer_sum(act_ref[x, :, cols], up_ref[y])

    gain_x.wait_recv()
    gain_mid[...] = gain_ref[...] + gain_in[0]
    act_x.wait_recv()
    act_d.start()
    up_y.wait_recv()
    up_d.start()
    gain_y.start()

    def add_source(slot):
        @pl.loop(0, planes)
        def _(b):
            cols = pl.ds(pl.multiple_of(b * rows, 128), rows)
            part[b] += outer_sum(gath_a[slot, :, cols], gath_u[slot])

    up_x.wait_recv()
    add_source(0)
    act_y.wait_recv()
    add_source(1)
    gain_y.wait_recv()
    gain_sum[...] = gain_mid[...] + gain_in[1]
    gain_zs = [
        copy(gain_sum, gain_z.at[step], g_send.at[2 + step], g_recv.at[2 + step], z_peers[step])
        for step in range(planes - 1)
    ]
    for tiny in gain_zs:
        tiny.start()
    act_d.wait_recv()
    up_d.wait_recv()
    add_source(2)

    z_next = lax.rem(me + 4, total)
    z_prev = lax.rem(me + total - 4, total)

    def right(b):
        return copy(to_right.at[b], from_left.at[b], r_send.at[b], r_recv.at[b], z_next)

    def left(b):
        return copy(to_left.at[b], from_right.at[b], l_send.at[b], l_recv.at[b], z_prev)

    for t in range(planes - 1):
        @pl.when(t >= z)
        def _():
            b = planes - 1 - t + z

            @pl.when(z > 0)
            def _():
                right(b).wait_recv()
                to_right[b] = (part[b] + from_left[b].astype(F32)).astype(BF16)

            @pl.when(z == 0)
            def _():
                to_right[b] = part[b].astype(BF16)

            right(b).start()

        @pl.when(t >= planes - 1 - z)
        def _():
            b = t - (planes - 1 - z)

            @pl.when(z < planes - 1)
            def _():
                left(b).wait_recv()
                to_left[b] = (part[b] + from_right[b].astype(F32)).astype(BF16)

            @pl.when(z == planes - 1)
            def _():
                to_left[b] = part[b].astype(BF16)

            left(b).start()

    @pl.when(z > 0)
    def _():
        right(z).wait_recv()
        part[z] += from_left[z].astype(F32)

    @pl.when(z < planes - 1)
    def _():
        left(z).wait_recv()
        part[z] += from_right[z].astype(F32)

    other = pl.ds(pl.multiple_of((1 - y) * share, 64), share)
    own = pl.ds(pl.multiple_of(y * share, 64), share)
    swap_out[...] = part[z, other, :].astype(BF16)
    swap = copy(swap_out, swap_in, xy_send.at[6], xy_recv.at[6], yn)
    swap.start()

    for tiny in gain_zs:
        tiny.wait_recv()
    total_gain = gain_sum[...]
    for step in range(planes - 1):
        total_gain = total_gain + gain_z[step]
    gain_out[...] = total_gain

    @pl.when(y == 0)
    def _():
        out_ref[:, :half] = part[z, own, :]

    @pl.when(y == 1)
    def _():
        out_ref[:, half:] = part[z, own, :]

    swap.wait_recv()

    @pl.when(y == 0)
    def _():
        out_ref[:, half:] = swap_in[...].astype(F32)

    @pl.when(y == 1)
    def _():
        out_ref[:, :half] = swap_in[...].astype(F32)

    for sent in [gain_x, act_x, up_y, up_x, act_y, act_d, up_d, gain_y, swap] + gain_zs:
        sent.wait_send()
    for t in range(planes - 1):
        @pl.when(t >= z)
        def _():
            right(planes - 1 - t + z).wait_send()

        @pl.when(t >= planes - 1 - z)
        def _():
            left(t - (planes - 1 - z)).wait_send()


def reduce_weight(act2, up2, gain):
    count = lax.axis_size("dp")
    planes = count // 4
    _, tokens, half = act2.shape
    rows = half // planes
    share = rows // 2
    vmem = pl.BlockSpec(memory_space=pltpu.VMEM)
    block = (planes, rows, half)
    sems = pltpu.SemaphoreType.DMA
    return pl.pallas_call(
        functools.partial(weight_kernel, planes),
        out_shape=(
            jax.ShapeDtypeStruct((share, 2 * half), F32),
            jax.ShapeDtypeStruct(gain.shape, F32),
        ),
        in_specs=[vmem] * 3,
        out_specs=(vmem, vmem),
        scratch_shapes=[
            pltpu.VMEM((3, tokens, half), BF16),
            pltpu.VMEM((3, tokens, half), BF16),
            pltpu.VMEM(block, F32),
            pltpu.VMEM(block, BF16),
            pltpu.VMEM(block, BF16),
            pltpu.VMEM(block, BF16),
            pltpu.VMEM(block, BF16),
            pltpu.VMEM((share, half), BF16),
            pltpu.VMEM((share, half), BF16),
            pltpu.VMEM((2,) + gain.shape, F32),
            pltpu.VMEM(gain.shape, F32),
            pltpu.VMEM(gain.shape, F32),
            pltpu.VMEM((planes - 1,) + gain.shape, F32),
            sems((7,)), sems((7,)), sems((planes,)), sems((planes,)),
            sems((planes,)), sems((planes,)), sems((planes + 1,)), sems((planes + 1,)),
        ],
        compiler_params=pltpu.CompilerParams(
            collective_id=0, has_side_effects=True, vmem_limit_bytes=40 << 20
        ),
    )(act2, up2, gain)


def body(section_inputs, mix_weight, norm_gain, out_cotangent, positions):
    sections = lax.axis_size("section")
    section_id = lax.axis_index("section")
    micro, tok_mb, channels = section_inputs.shape[1:]
    tokens = micro * tok_mb
    count = lax.axis_size("dp")
    planes = count // 4
    share = channels // count
    inputs = section_inputs[0].reshape(tokens, channels).astype(F32)
    cot = out_cotangent.reshape(tokens, channels)
    factor = 1.0 + 0.5 * jnp.sin(2.0 * math.pi * positions.reshape(tokens, 1).astype(F32) / DEPTH)
    weight_mat = mix_weight[0]
    gain_vec = norm_gain[0]
    inv_rms = lax.rsqrt(jnp.mean(inputs * inputs, axis=-1, keepdims=True) + 1e-06)
    normed = inputs * inv_rms * gain_vec
    activation, gelu_back = jax.vjp(jax.nn.gelu, normed)
    slope = gelu_back(jnp.ones_like(normed))[0]
    act2 = (
        activation.astype(BF16)
        .reshape(tokens, planes, 2, 2, share)
        .transpose(3, 0, 1, 2, 4)
        .reshape(2, tokens, channels // 2)
    )
    act2, slope, inv_rms, factor = lax.optimization_barrier((act2, slope, inv_rms, factor))

    grad_out = cot
    for step in range(sections):
        upstream = (factor * grad_out.astype(F32)).astype(BF16)
        back = lax.dot_general(
            upstream, weight_mat, (((1,), (1,)), ((), ())), preferred_element_type=F32
        )
        grad_norm = back * slope
        scaled = grad_norm * gain_vec
        projected = jnp.mean(scaled * inputs, axis=-1, keepdims=True)
        delta = inv_rms * scaled - inputs * (inv_rms * inv_rms * inv_rms) * projected
        grad_in = (grad_out.astype(F32) + delta).astype(BF16)
        if step < sections - 1:
            pairs = [(s, s - 1) for s in range(1, sections)]
            received = lax.ppermute(grad_in, "section", pairs)
            grad_out = jnp.where(section_id == sections - 1, cot, received)
    gain_term = jnp.sum(grad_norm * inputs * inv_rms, axis=0)[None]
    up2 = upstream.reshape(tokens, 2, channels // 2).transpose(1, 0, 2)
    weight_grad, gain_all = reduce_weight(act2, up2, gain_term)
    gain_share = lax.dynamic_slice_in_dim(gain_all[0], lax.axis_index("dp") * share, share, 0)
    return (grad_in.reshape(1, micro, tok_mb, channels), weight_grad[None], gain_share[None])


def solution(mesh):
    return jax.shard_map(
        body,
        mesh=mesh,
        in_specs=(
            P("section", None, "dp", None),
            P("section", None, None),
            P("section", None),
            P(None, "dp", None),
            P(None, "dp"),
        ),
        out_specs=(P("section", None, "dp", None), P("section", "dp", None), P("section", "dp")),
        check_vma=False,
    )
```

time: 460 us -> 129 us (0.28)
  waiting for transfers between devices: 299 us -> 3.4 us
  Pallas kernels: 0 us -> 81.7 us
  blocking collectives: 57.9 us -> 0 us
  local copies, waits for them, and re-layouts: 30 us -> 13.6 us
  between operations: 14.8 us -> 0.8 us
  matrix products: 26.6 us -> 14 us
  other arithmetic: 22.5 us -> 13.7 us
    unnamed x2 -> x0, waiting for transfers between devices: 291 us -> none
    pallas_call x0 -> x1, Pallas kernels: none -> 81.7 us  [reduce_weight(): pl.pallas_call(functools.partial(weight_kernel, planes), out_shape=(jax.S...]
    unnamed x1 -> x0, blocking collectives: 57.9 us -> none
    unnamed x6 -> x15, local copies, waits for them, and re-layouts: 24.9 us -> 2.32 us
    dot_general x5 -> x2, matrix products: 26.6 us -> 14 us  [body(): lax.dot_general(upstream, weight_mat, (((1,), (1,)), ((), ())), preferred...]
    dynamic_update_slice x6 -> x0, other arithmetic: 10.3 us -> none  [the longest x3 6.08 us: tick(): lax.dynamic_update_slice_in_dim(grads, jnp.where(active, grad_in, old_gra...]
    convert_element_type x0 -> x4, other arithmetic: none -> 8.02 us  [the longest x2 5.28 us: body(): grad_in = (grad_out.astype(F32) + delta).astype(BF16)]
    concatenate x1 -> x0, other arithmetic: 7.5 us -> none  [body(): jnp.concatenate(blocks, axis=1).astype(jnp.bfloat16)]
  transfers between devices with their start and end apart: 4 -> 1, of which waited for: 4 -> 1; matrix products, arithmetic and copies ran while one was open for 0% -> 0% of each run, Pallas kernels for 0% -> 0%
where the time goes in v1:
time: 129 us
  Pallas kernels  81.7 us (63%)
  matrix products  14 us (11%)
  other arithmetic  13.7 us (11%)
  local copies, waits for them, and re-layouts  13.6 us (11%)
  waiting for transfers between devices  3.4 us (3%)
  starting transfers between devices  1.46 us (1%)
    pallas_call x1, Pallas kernels, reduce_weight(): pl.pallas_call(functools.partial(weight_kernel, planes), out_shape=(jax.S...  81.7 us
    dot_general x2, matrix products, body(): lax.dot_general(upstream, weight_mat, (((1,), (1,)), ((), ())), preferred...  14 us
    convert_element_type x2, other arithmetic, body(): grad_in = (grad_out.astype(F32) + delta).astype(BF16)  5.28 us
    ppermute x1, waiting for transfers between devices, body(): received = lax.ppermute(grad_in, 'section', pairs)  3.4 us
    convert_element_type x1, local copies, waits for them, and re-layouts, body(): inputs = section_inputs[0].reshape(tokens, channels).astype(F32)  3.16 us
    add_any x1, other arithmetic, body(): activation, gelu_back = jax.vjp(jax.nn.gelu, normed)  2.85 us
    convert_element_type x2, other arithmetic, body(): upstream = (factor * grad_out.astype(F32)).astype(BF16)  2.74 us
  transfers between devices with their start and end apart: 1, of which 1 were waited for; matrix products, arithmetic and copies ran while one was open for 0% of the time, Pallas kernels for 0%

profile of v1, /device:TPU:0, one launch (start us, length us, event | category | flops | bytes accessed | tf_op | source)
XLA Modules:
  0.0 128.6 jit_solution(16295707126090365230)
XLA Ops:
  0.6 0.0 copy-start
  0.7 1.6 %fusion.35 = f32[2,128]{1,0:T(2,128)S(1)} fusion(bf16[1,2,128,2048]{3,2,1,0:T(8,128)(2,1)} %param.5), kind=kLoop, calls=%fused_computation.40 | loop fusion | flops 1572608 | bytes 1049600 | tf_op jit(solution)/shard_map/reduce_sum | solution.py:243
  2.3 3.2 %reshape.122 = f32[256,4,2,2,128]{4,3,2,1,0:T(2,128)S(1)} reshape(bf16[1,2,128,2048]{3,2,1,0:T(8,128)(2,1)} %param.5) | data formatting | bytes 3145728 | tf_op jit(solution)/shard_map/convert_element_type | solution.py:238
  5.4 0.0 copy-done.6
  5.5 2.8 %fusion.20 = f32[256,2048]{1,0:T(8,128)} fusion(bf16[1,2,128,2048]{3,2,1,0:T(8,128)(2,1)S(1)} %copy-done, f32[2048]{0:T(1024)S(1)} %bitcast.92, f32[256]{0:T(256)S(1)} %get-tuple-element.18), kind=kLoop, calls=%fused_computation.19 | loop fusion | flops 10485760 | bytes 3154944 | tf_op jit(solution)/shard_map/transpose(jvp())/add_any | solution.py:245
  8.4 1.1 fusion.44
  9.5 0.0 copy-start.1
  9.5 2.0 %copy.18 = bf16[2,256,4,2,128]{4,3,2,1,0:T(2,128)(2,1)} copy(bf16[2,256,4,2,128]{4,1,0,3,2:T(8,128)(2,1)S(1)} %fusion.44) | data formatting | bytes 2097152 | tf_op jit(solution)/shard_map/transpose | solution.py:250
  11.6 1.8 %reshape.119.act_ref = bf16[2,256,1024]{2,1,0:T(8,128)(2,1)S(1)} reshape(bf16[2,256,4,2,128]{4,3,2,1,0:T(2,128)(2,1)} %copy.18) | data formatting | bytes 2097152 | tf_op jit(solution)/shard_map/reshape | solution.py:251
  13.4 0.2 multiply_convert_fusion
  13.6 1.3 %copy-done.3 = f32[256,2048]{1,0:T(8,128)S(1)} copy-done((f32[256,2048]{1,0:T(8,128)S(1)}, f32[256,2048]{1,0:T(8,128)}, u32[]{:S(2)}) %copy-start.3) | copy-done | bytes 2097176
  14.9 6.1 %fusion.39 = (f32[256]{0:T(256)S(1)}, f32[256,2048]{1,0:T(8,128)S(1)}) fusion(bf16[1,2,128,2048]{3,2,1,0:T(8,128)(2,1)S(1)} %copy-done, f32[2048]{0:T(1024)S(1)} %bitcast.94, f32[256,2048]{1,0:T(8,128)S(1)} %copy-done.3, bf16[256,2048]{1,0:T(8,128)(2,1)S(1)} %bitcast.91, bf16[1,2048,2048]{2,1,0:T(8,128)(2,1)} %param.6), kind=kOutput, calls=%fused_computation.44 | convolution fusion | flops 2150104832 | bytes 14689280 | tf_op jit(solution)/shard_map/dot_general | solution.py:258
  21.1 1.6 %fusion.33 = bf16[256,2048]{1,0:T(8,128)(2,1)} fusion(bf16[1,2,128,2048]{3,2,1,0:T(8,128)(2,1)S(1)} %copy-done, f32[256,2048]{1,0:T(8,128)S(1)} %get-tuple-element.20, bf16[2,128,2048]{2,1,0:T(8,128)(2,1)S(1)} %copy-done.1, f32[256]{0:T(256)S(1)} %broadcast_multiply_fusion.1, f32[256]{0:T(256)S(1)} %bitcast.102, f32[256]{0:T(256)S(1)} %bitcast.98), kind=kLoop, calls=%fused_computation.38 | loop fusion | flops 4194304 | bytes 5245952 | tf_op jit(solution)/shard_map/convert_element_type | solution.py:265
  22.7 1.5 %collective-permute-start = (bf16[256,2048]{1,0:T(8,128)(2,1)}, bf16[256,2048]{1,0:T(8,128)(2,1)}, u32[]{:S(2)}, u32[]{:S(2)}) collective-permute-start(bf16[256,2048]{1,0:T(8,128)(2,1)} %fusion.33), channel_id=1, source_target_pairs={{1,0},{3,2},{5,4},{7,6},{9,8},{11,10},{13,12},{15,14},{17,16},{19,... | collective-permute-start | bytes 3145736 | tf_op jit(solution)/shard_map/ppermute | solution.py:268
  24.2 3.4 %collective-permute-done = bf16[256,2048]{1,0:T(8,128)(2,1)} collective-permute-done((bf16[256,2048]{1,0:T(8,128)(2,1)}, bf16[256,2048]{1,0:T(8,128)(2,1)}, u32[]{:S(2)}, u32[]{:S(2)}) %collective-permute-start) | collective-permute-done | bytes 1048608 | tf_op jit(solution)/shard_map/ppermute | solution.py:268
  27.6 2.5 %fusion.13 = bf16[256,2048]{1,0:T(8,128)(2,1)} fusion(f32[256]{0:T(256)S(1)} %bitcast.101, bf16[256,2048]{1,0:T(8,128)(2,1)} %collective-permute-done, bf16[2,128,2048]{2,1,0:T(8,128)(2,1)S(1)} %copy-done.1, pred[]{:T(512)S(6)} %eq.3), kind=kLoop, calls=%fused_computation.12 | loop fusion | flops 2097152 | bytes 3146753 | tf_op jit(solution)/shard_map/convert_element_type | solution.py:257
  30.1 7.9 %fusion.42 = (f32[2048]{0:T(1024)S(1)}, f32[256]{0:T(256)S(1)}, f32[256,2048]{1,0:T(8,128)}) fusion(bf16[1,2,128,2048]{3,2,1,0:T(8,128)(2,1)S(1)} %copy-done, f32[256]{0:T(256)S(1)} %bitcast.99, f32[2048]{0:T(1024)S(1)} %bitcast.95, f32[256,2048]{1,0:T(8,128)S(1)} %copy-done.4, bf16[256,2048]{1,0:T(8,128)(2,1)} %fusion.13, bf16[1,2048,2048]{2,1,0:T(8,128)(2,1)} %param.6), kind=kOutput, calls=%fused_computation.47 | convolution fusion | flops 2151675648 | bytes 14698496 | tf_op jit(solution)/shard_map/dot_general | solution.py:258
  38.0 2.3 %copy.19 = bf16[256,2048]{0,1:T(8,128)(2,1)} copy(bf16[256,2048]{1,0:T(8,128)(2,1)} %fusion.13) | data formatting | bytes 2097152 | tf_op jit(solution)/shard_map/convert_element_type | solution.py:257
  40.3 1.5 %copy.20 = bf16[256,2,1024]{2,0,1:T(8,128)(2,1)S(1)} copy(bf16[256,2,1024]{0,2,1:T(8,128)(2,1)} %bitcast.89) | data formatting | bytes 2097152 | tf_op jit(solution)/shard_map/reshape | solution.py:271
  41.8 0.0 copy-start.2
  41.8 81.7 %shard_map.76 = (f32[128,2048]{1,0:T(8,128)S(1)}, f32[1,2048]{1,0:T(1,128)S(1)}) custom-call(bf16[2,256,1024]{2,1,0:T(8,128)(2,1)S(1)} %reshape.119.act_ref, bf16[2,256,1024]{2,1,0:T(8,128)(2,1)S(1)} %bitcast.86, f32[1,2048]{1,0:T(1,128)S(1)} %bitcast.88), custom_call_target="tpu_custom_call" | custom-call | tf_op jit(solution)/shard_map/pallas_call | solution.py:199
  123.5 0.5 constant_dynamic-slice_fusion
  124.0 3.6 %fusion.14 = bf16[256,2048]{1,0:T(8,128)(2,1)} fusion(bf16[1,2,128,2048]{3,2,1,0:T(8,128)(2,1)S(1)} %copy-done, f32[256,2048]{1,0:T(8,128)} %get-tuple-element.21, f32[256]{0:T(256)S(1)} %broadcast_multiply_fusion, f32[256]{0:T(256)S(1)} %bitcast.103, f32[256]{0:T(256)S(1)} %bitcast.100, f32[2048]{0:T(1024)S(1)} %bitcast.96, ...), kind=kLoop, calls=%fused_computation.13 | loop fusion | flops 5242880 | bytes 6302721 | tf_op jit(solution)/shard_map/convert_element_type | solution.py:265
  127.7 1.0 copy.29
  (14 shorter events, 0.1 us)
Async XLA Ops:
  0.6 4.9 %copy-start = (bf16[1,2,128,2048]{3,2,1,0:T(8,128)(2,1)S(1)}, bf16[1,2,128,2048]{3,2,1,0:T(8,128)(2,1)}, u32[]{:S(2)}) copy-start(bf16[1,2,128,2048]{3,2,1,0:T(8,128)(2,1)} %param.5) | copy-start | bytes 3145732
  0.6 4.8 %copy-start.6 = (s32[2,128]{1,0:T(2,128)S(1)}, s32[2,128]{1,0:T(2,128)}, u32[]{:S(2)}) copy-start(s32[2,128]{1,0:T(2,128)} %param.9) | copy-start | bytes 3076
  0.7 4.9 %copy-start.5 = (f32[1,2048]{1,0:T(1,128)S(1)}, f32[1,2048]{1,0:T(1,128)}, u32[]{:S(2)}) copy-start(f32[1,2048]{1,0:T(1,128)} %param.7) | copy-start | bytes 24580
  9.5 3.9 %copy-start.1 = (bf16[2,128,2048]{2,1,0:T(8,128)(2,1)S(1)}, bf16[2,128,2048]{2,1,0:T(8,128)(2,1)}, u32[]{:S(2)}) copy-start(bf16[2,128,2048]{2,1,0:T(8,128)(2,1)} %param.8) | copy-start | bytes 3145732
  13.4 1.6 %copy-start.3 = (f32[256,2048]{1,0:T(8,128)S(1)}, f32[256,2048]{1,0:T(8,128)}, u32[]{:S(2)}) copy-start(f32[256,2048]{1,0:T(8,128)} %fusion.20) | copy-start | bytes 6291460
  22.7 4.9 %collective-permute-start = (bf16[256,2048]{1,0:T(8,128)(2,1)}, bf16[256,2048]{1,0:T(8,128)(2,1)}, u32[]{:S(2)}, u32[]{:S(2)}) collective-permute-start(bf16[256,2048]{1,0:T(8,128)(2,1)} %fusion.33), channel_id=1, source_target_pairs={{1,0},{3,2},{5,4},{7,6},{9,8},{11,10},{13,12},{15,14},{17,16},{19,... | collective-permute-start | bytes 3145736 | tf_op jit(solution)/shard_map/ppermute | solution.py:268
  24.2 5.9 %copy-start.4 = (f32[256,2048]{1,0:T(8,128)S(1)}, f32[256,2048]{1,0:T(8,128)}, u32[]{:S(2)}) copy-start(f32[256,2048]{1,0:T(8,128)} %fusion.20) | copy-start | bytes 6291460
  41.8 82.2 %copy-start.2 = (bf16[2,128,2048]{2,1,0:T(8,128)(2,1)S(1)}, bf16[2,128,2048]{2,1,0:T(8,128)(2,1)}, u32[]{:S(2)}) copy-start(bf16[2,128,2048]{2,1,0:T(8,128)(2,1)} %param.8) | copy-start | bytes 3145732

commit v2 on v1

v2 whole, which is shorter than its diff:
```python
import functools
import math

import jax
import jax.numpy as jnp
from jax import lax
from jax.experimental import pallas as pl
from jax.experimental.pallas import tpu as pltpu
from jax.sharding import PartitionSpec as P

DEPTH = 1024
MESH = pl.DeviceIdType.MESH
F32 = jnp.float32
BF16 = jnp.bfloat16


def outer_sum(a, b):
    return lax.dot_general(a, b, (((0,), (0,)), ((), ())), preferred_element_type=F32)


ROOT = math.sqrt(2.0 / math.pi)
CUBE = 0.044715


def back_kernel(
    planes, sections, x_hbm, w_hbm, cot_hbm, gain_ref, factor_ref, out_ref, gain_out, grads_ref,
    x_ref, w_ref, g_ref, slope, act_ref, up_ref, q_ref, m_ref, proj,
    gath_a, gath_u, part, from_left, from_right, to_right, to_left, swap_out, swap_in,
    gain_own, gain_in, gain_mid, gain_sum, gain_z,
    in_sem, sec_send, sec_recv,
    xy_send, xy_recv, r_send, r_recv, l_send, l_recv, g_send, g_recv,
):
    me = lax.axis_index("dp")
    sec = lax.axis_index("section")
    last = sections - 1
    total = planes * 4
    x = lax.rem(me, 2)
    y = lax.rem(me // 2, 2)
    z = me // 4
    xn = me + 1 - 2 * x
    yn = me + 2 - 4 * y
    tokens, channels = x_ref.shape
    half = channels // 2
    rows = half // planes
    share = rows // 2
    micro, tok_mb = factor_ref.shape
    step_rows = 16
    width = min(256, channels)

    load_x = pltpu.make_async_copy(x_hbm, x_ref, in_sem.at[0])
    load_w = pltpu.make_async_copy(w_hbm, w_ref, in_sem.at[1])
    load_g = pltpu.make_async_copy(cot_hbm, g_ref, in_sem.at[2])
    load_x.start()

    def copy(src, dst, send, recv, to):
        return pltpu.make_async_remote_copy(
            src_ref=src, dst_ref=dst, send_sem=send, recv_sem=recv,
            device_id={"dp": to}, device_id_type=MESH,
        )

    barrier = pltpu.get_barrier_semaphore()
    z_peers = [lax.rem(me + 4 * step, total) for step in range(1, planes)]
    for peer in [xn, yn] + z_peers:
        pl.semaphore_signal(barrier, inc=1, device_id={"dp": peer}, device_id_type=MESH)

    @pl.when(sec > 0)
    def _():
        pl.semaphore_signal(barrier, inc=1, device_id={"section": sec - 1}, device_id_type=MESH)

    @pl.when(sec < last)
    def _():
        pl.semaphore_signal(barrier, inc=1, device_id={"section": sec + 1}, device_id_type=MESH)

    @pl.when(sec == last)
    def _():
        load_g.start()

    load_w.start()

    for mb in range(micro):
        m_ref[mb * tok_mb:(mb + 1) * tok_mb, :] = jnp.transpose(
            jnp.broadcast_to(factor_ref[mb:mb + 1, :], (128, tok_mb))
        )
    proj[...] = jnp.zeros_like(proj)
    load_x.wait()

    @pl.loop(0, tokens // step_rows)
    def _(i):
        r = pl.ds(pl.multiple_of(i * step_rows, step_rows), step_rows)
        square = jnp.zeros((step_rows, rows), F32)
        for c in range(channels // rows):
            xc = x_ref[r, c * rows:(c + 1) * rows].astype(F32)
            square = square + xc * xc
        q = lax.rsqrt(jnp.sum(square, axis=-1, keepdims=True) / channels + 1e-06)
        q_ref[r, :] = jnp.broadcast_to(q, (step_rows, 128))
        for c in range(channels // rows):
            cols = slice(c * rows, (c + 1) * rows)
            n = x_ref[r, cols].astype(F32) * q * gain_ref[:, cols]
            n2 = n * n
            th = jnp.tanh(ROOT * (n + CUBE * (n2 * n)))
            cdf = 0.5 * (1.0 + th)
            act_ref[c % 2, r, (c // 2) * rows:(c // 2 + 1) * rows] = (n * cdf).astype(BF16)
            slope[r, cols] = cdf + (0.5 * ROOT) * n * (1.0 - th * th) * (1.0 + (3.0 * CUBE) * n2)

    beside = jnp.minimum(sec, 1) + jnp.minimum(last - sec, 1)
    pl.semaphore_wait(barrier, 1 + planes + beside)

    act_y = copy(act_ref.at[1 - y], gath_a.at[1], xy_send.at[0], xy_recv.at[0], yn)
    act_x = copy(act_ref.at[y], gath_a.at[0], xy_send.at[1], xy_recv.at[1], xn)
    up_x = copy(up_ref.at[1 - x], gath_u.at[0], xy_send.at[2], xy_recv.at[2], xn)
    up_y = copy(up_ref.at[x], gath_u.at[1], xy_send.at[3], xy_recv.at[3], yn)
    act_d = copy(gath_a.at[1], gath_a.at[2], xy_send.at[4], xy_recv.at[4], xn)
    up_d = copy(gath_u.at[0], gath_u.at[2], xy_send.at[5], xy_recv.at[5], yn)
    gain_x = copy(gain_own, gain_in.at[0], g_send.at[0], g_recv.at[0], xn)
    gain_y = copy(gain_mid, gain_in.at[1], g_send.at[1], g_recv.at[1], yn)
    act_y.start()
    act_x.start()

    def relay(mb):
        span = pl.ds(mb * tok_mb, tok_mb)
        return pltpu.make_async_remote_copy(
            src_ref=grads_ref.at[span, :], dst_ref=g_ref.at[span, :],
            send_sem=sec_send.at[mb], recv_sem=sec_recv.at[mb],
            device_id={"section": jnp.maximum(sec - 1, 0)}, device_id_type=MESH,
        )

    @pl.when(sec < last)
    def _():
        act_y.wait_recv()
        act_d.start()

    @pl.when(sec == last)
    def _():
        load_g.wait()

    for mb in range(micro):
        @pl.when(sec < last)
        def _():
            relay(mb).wait_recv()

        @pl.loop(mb * (tok_mb // step_rows), (mb + 1) * (tok_mb // step_rows))
        def _(i):
            r = pl.ds(pl.multiple_of(i * step_rows, step_rows), step_rows)
            m = m_ref[r, :1]
            for h in range(2):
                g = g_ref[r, h * half:(h + 1) * half].astype(F32)
                up_ref[h, r, :] = (m * g).astype(BF16)

    up_x.start()
    up_y.start()
    load_w.wait()

    @pl.loop(0, channels // width)
    def _(c):
        cols = pl.ds(pl.multiple_of(c * width, width), width)
        last_dims = (((1,), (1,)), ((), ()))
        back = lax.dot_general(
            up_ref[0], w_ref[cols, :half], last_dims, preferred_element_type=F32
        ) + lax.dot_general(up_ref[1], w_ref[cols, half:], last_dims, preferred_element_type=F32)
        grad_norm = back * slope[:, cols]
        xc = x_ref[:, cols].astype(F32)
        scaled = grad_norm * gain_ref[:, cols]
        slope[:, cols] = scaled
        along = scaled * xc
        lanes = proj[...]
        for k in range(width // 128):
            lanes = lanes + along[:, k * 128:(k + 1) * 128]
        proj[...] = lanes
        gain_own[:, cols] = jnp.sum(grad_norm * xc * q_ref[:, :1], axis=0, keepdims=True)

    for mb in range(micro):
        @pl.loop(mb * (tok_mb // step_rows), (mb + 1) * (tok_mb // step_rows))
        def _(i):
            r = pl.ds(pl.multiple_of(i * step_rows, step_rows), step_rows)
            q = q_ref[r, :1]
            pull = (q * q * q) * (jnp.sum(proj[r, :], axis=-1, keepdims=True) / channels)
            for c in range(channels // width):
                cols = slice(c * width, (c + 1) * width)
                delta = q * slope[r, cols] - x_ref[r, cols].astype(F32) * pull
                grads_ref[r, cols] = (g_ref[r, cols].astype(F32) + delta).astype(BF16)

        @pl.when(sec > 0)
        def _():
            relay(mb).start()

    @pl.when(sec == last)
    def _():
        act_y.wait_recv()
        act_d.start()

    up_x.wait_recv()
    up_d.start()
    gain_x.start()

    @pl.loop(0, planes)
    def _(b):
        cols = pl.ds(pl.multiple_of(b * rows, 128), rows)
        part[b] = outer_sum(act_ref[y, :, cols], up_ref[x])

    def add_source(slot):
        @pl.loop(0, planes)
        def _(b):
            cols = pl.ds(pl.multiple_of(b * rows, 128), rows)
            part[b] += outer_sum(gath_a[slot, :, cols], gath_u[slot])

    act_x.wait_recv()
    add_source(0)
    up_y.wait_recv()
    add_source(1)
    gain_x.wait_recv()
    gain_mid[...] = gain_own[...] + gain_in[0]
    gain_y.start()
    act_d.wait_recv()
    up_d.wait_recv()
    add_source(2)
    gain_y.wait_recv()
    gain_sum[...] = gain_mid[...] + gain_in[1]
    gain_zs = [
        copy(gain_sum, gain_z.at[step], g_send.at[2 + step], g_recv.at[2 + step], z_peers[step])
        for step in range(planes - 1)
    ]
    for tiny in gain_zs:
        tiny.start()

    z_next = lax.rem(me + 4, total)
    z_prev = lax.rem(me + total - 4, total)

    def right(b):
        return copy(to_right.at[b], from_left.at[b], r_send.at[b], r_recv.at[b], z_next)

    def left(b):
        return copy(to_left.at[b], from_right.at[b], l_send.at[b], l_recv.at[b], z_prev)

    for t in range(planes - 1):
        @pl.when(t >= z)
        def _():
            b = planes - 1 - t + z

            @pl.when(z > 0)
            def _():
                right(b).wait_recv()
                to_right[b] = (part[b] + from_left[b].astype(F32)).astype(BF16)

            @pl.when(z == 0)
            def _():
                to_right[b] = part[b].astype(BF16)

            right(b).start()

        @pl.when(t >= planes - 1 - z)
        def _():
            b = t - (planes - 1 - z)

            @pl.when(z < planes - 1)
            def _():
                left(b).wait_recv()
                to_left[b] = (part[b] + from_right[b].astype(F32)).astype(BF16)

            @pl.when(z == planes - 1)
            def _():
                to_left[b] = part[b].astype(BF16)

            left(b).start()

    @pl.when(z > 0)
    def _():
        right(z).wait_recv()
        part[z] += from_left[z].astype(F32)

    @pl.when(z < planes - 1)
    def _():
        left(z).wait_recv()
        part[z] += from_right[z].astype(F32)

    other = pl.ds(pl.multiple_of((1 - x) * share, 64), share)
    own = pl.ds(pl.multiple_of(x * share, 64), share)
    swap_out[...] = part[z, other, :].astype(BF16)
    swap = copy(swap_out, swap_in, xy_send.at[6], xy_recv.at[6], xn)
    swap.start()

    for tiny in gain_zs:
        tiny.wait_recv()
    total_gain = gain_sum[...]
    for step in range(planes - 1):
        total_gain = total_gain + gain_z[step]
    gain_out[...] = total_gain

    @pl.when(x == 0)
    def _():
        out_ref[:, :half] = part[z, own, :]

    @pl.when(x == 1)
    def _():
        out_ref[:, half:] = part[z, own, :]

    swap.wait_recv()

    @pl.when(x == 0)
    def _():
        out_ref[:, half:] = swap_in[...].astype(F32)

    @pl.when(x == 1)
    def _():
        out_ref[:, :half] = swap_in[...].astype(F32)

    for sent in [gain_x, act_x, up_y, up_x, act_y, act_d, up_d, gain_y, swap] + gain_zs:
        sent.wait_send()
    for t in range(planes - 1):
        @pl.when(t >= z)
        def _():
            right(planes - 1 - t + z).wait_send()

        @pl.when(t >= planes - 1 - z)
        def _():
            left(t - (planes - 1 - z)).wait_send()

    @pl.when(sec > 0)
    def _():
        for mb in range(micro):
            relay(mb).wait_send()


def body(section_inputs, mix_weight, norm_gain, out_cotangent, positions):
    sections = lax.axis_size("section")
    micro, tok_mb, channels = section_inputs.shape[1:]
    tokens = micro * tok_mb
    count = lax.axis_size("dp")
    planes = count // 4
    share = channels // count
    half = channels // 2
    rows = half // planes
    factor = 1.0 + 0.5 * jnp.sin(2.0 * math.pi * positions.astype(F32) / DEPTH)
    vmem = pl.BlockSpec(memory_space=pltpu.VMEM)
    hbm = pl.BlockSpec(memory_space=pl.ANY)
    block = (planes, rows, half)
    line = (1, channels)
    sems = pltpu.SemaphoreType.DMA
    weight_grad, gain_all, grads = pl.pallas_call(
        functools.partial(back_kernel, planes, sections),
        out_shape=(
            jax.ShapeDtypeStruct((share, channels), F32),
            jax.ShapeDtypeStruct(line, F32),
            jax.ShapeDtypeStruct((tokens, channels), BF16),
        ),
        in_specs=[hbm, hbm, hbm, vmem, vmem],
        out_specs=(vmem, vmem, vmem),
        scratch_shapes=[
            pltpu.VMEM((tokens, channels), BF16),
            pltpu.VMEM((channels, channels), BF16),
            pltpu.VMEM((tokens, channels), BF16),
            pltpu.VMEM((tokens, channels), F32),
            pltpu.VMEM((2, tokens, half), BF16),
            pltpu.VMEM((2, tokens, half), BF16),
            pltpu.VMEM((tokens, 128), F32),
            pltpu.VMEM((tokens, 128), F32),
            pltpu.VMEM((tokens, 128), F32),
            pltpu.VMEM((3, tokens, half), BF16),
            pltpu.VMEM((3, tokens, half), BF16),
            pltpu.VMEM(block, F32),
            pltpu.VMEM(block, BF16),
            pltpu.VMEM(block, BF16),
            pltpu.VMEM(block, BF16),
            pltpu.VMEM(block, BF16),
            pltpu.VMEM((share, half), BF16),
            pltpu.VMEM((share, half), BF16),
            pltpu.VMEM(line, F32),
            pltpu.VMEM((2,) + line, F32),
            pltpu.VMEM(line, F32),
            pltpu.VMEM(line, F32),
            pltpu.VMEM((planes - 1,) + line, F32),
            sems((3,)), sems((micro,)), sems((micro,)),
            sems((7,)), sems((7,)), sems((planes,)), sems((planes,)),
            sems((planes,)), sems((planes,)), sems((planes + 1,)), sems((planes + 1,)),
        ],
        compiler_params=pltpu.CompilerParams(
            collective_id=0, has_side_effects=True, vmem_limit_bytes=56 << 20
        ),
    )(
        section_inputs.reshape(tokens, channels),
        mix_weight[0],
        out_cotangent.reshape(tokens, channels),
        norm_gain,
        factor,
    )
    gain_share = lax.dynamic_slice_in_dim(gain_all[0], lax.axis_index("dp") * share, share, 0)
    return (grads.reshape(1, micro, tok_mb, channels), weight_grad[None], gain_share[None])


def solution(mesh):
    return jax.shard_map(
        body,
        mesh=mesh,
        in_specs=(
            P("section", None, "dp", None),
            P("section", None, None),
            P("section", None),
            P(None, "dp", None),
            P(None, "dp"),
        ),
        out_specs=(P("section", None, "dp", None), P("section", "dp", None), P("section", "dp")),
        check_vma=False,
    )
```

time: 129 us -> 99.7 us (0.77)
  matrix products: 14 us -> 0 us
  other arithmetic: 13.7 us -> 1.29 us
  Pallas kernels: 81.7 us -> 91.7 us
  local copies, waits for them, and re-layouts: 13.6 us -> 5.75 us
  waiting for transfers between devices: 3.4 us -> 0 us
  starting transfers between devices: 1.46 us -> 0 us
    dot_general x2 -> x0, matrix products: 14 us -> none  [body(): lax.dot_general(upstream, weight_mat, (((1,), (1,)), ((), ())), preferred...]
    pallas_call x1, Pallas kernels: 81.7 us -> 91.7 us  [body(): pl.pallas_call(functools.partial(back_kernel, planes, sections), out_shap...]
    convert_element_type x4 -> x0, other arithmetic: 8.02 us -> none  [the longest x2 5.28 us: body(): grad_in = (grad_out.astype(F32) + delta).astype(BF16)]
    convert_element_type x2 -> x0, local copies, waits for them, and re-layouts: 5.42 us -> none  [the longest x1 3.16 us: body(): inputs = section_inputs[0].reshape(tokens, channels).astype(F32)]
    ppermute x1 -> x0, waiting for transfers between devices: 3.4 us -> none  [body(): received = lax.ppermute(grad_in, 'section', pairs)]
    reshape x2 -> x0, local copies, waits for them, and re-layouts: 3.27 us -> none  [the longest x1 1.79 us: body(): act2 = activation.astype(BF16).reshape(tokens, planes, 2, 2, share).trans...]
    add_any x1 -> x0, other arithmetic: 2.85 us -> none  [body(): activation, gelu_back = jax.vjp(jax.nn.gelu, normed)]
    unnamed x15 -> x2, local copies, waits for them, and re-layouts: 2.32 us -> 4.6 us
  transfers between devices with their start and end apart: 1 -> 0, of which waited for: 1 -> 0; matrix products, arithmetic and copies ran while one was open for 0% -> 0% of each run, Pallas kernels for 0% -> 0%
where the time goes in v2:
time: 99.7 us; the launch traced here: 99.4 us
  Pallas kernels  91.7 us (92%)
  local copies, waits for them, and re-layouts  5.75 us (6%)
  other arithmetic  1.29 us (1%)
    pallas_call x1, Pallas kernels, body(): pl.pallas_call(functools.partial(back_kernel, planes, sections), out_shap...  91.7 us
    unnamed x2, local copies, waits for them, and re-layouts  4.6 us

profile of v2, /device:TPU:0, one launch (start us, length us, event | category | flops | bytes accessed | tf_op | source)
XLA Modules:
  0.0 99.4 jit_solution(10090225704544855678)
XLA Ops:
  0.6 1.3 %multiply_add_fusion.factor_ref = f32[2,128]{1,0:T(2,128)} fusion(s32[2,128]{1,0:T(2,128)} %param.9), kind=kLoop, calls=%fused_computation | loop fusion | flops 1024 | bytes 2048 | tf_op jit(solution)/shard_map/add | solution.py:332
  1.9 91.7 %shard_map.76 = (f32[128,2048]{1,0:T(8,128)}, f32[1,2048]{1,0:T(1,128)}, bf16[256,2048]{1,0:T(8,128)(2,1)}) custom-call(bf16[256,2048]{1,0:T(8,128)(2,1)} %bitcast.6, bf16[2048,2048]{1,0:T(8,128)(2,1)} %bitcast.5, bf16[256,2048]{1,0:T(8,128)(2,1)} %bitcast.7, f32[1,2048]{1,0:T(1,128)} %gain_ref.1, f32[2,128]{1,0:T(2,128)} %multiply_add_fusion.factor_ref), custom_call_target="tpu_custom_call" | custom-call | tf_op jit(solution)/shard_map/pallas_call | solution.py:338
  93.6 1.2 %constant_dynamic-slice_fusion = f32[1,128]{1,0:T(1,128)} fusion(f32[1,2048]{1,0:T(1,128)} %get-tuple-element.8, s32[]{:T(128)S(6)} %select_n.3), kind=kLoop, calls=%fused_computation.1 | loop fusion | bytes 1028 | tf_op jit(solution)/shard_map/dynamic_slice | solution.py:385
  94.8 2.3 %copy.10 = bf16[1,2,128,2048]{3,2,1,0:T(8,128)(2,1)} copy(bf16[1,2,128,2048]{3,2,1,0:T(8,128)(2,1)} %bitcast.9) | data formatting | bytes 2097152
  97.1 2.3 %copy.11 = f32[1,128,2048]{2,1,0:T(8,128)} copy(f32[1,128,2048]{2,1,0:T(8,128)} %bitcast.8) | data formatting | bytes 2097152

commit v3 on v2

--- a/solution.py
+++ b/solution.py
@@ -20,6 +20,7 @@
 
 ROOT = math.sqrt(2.0 / math.pi)
 CUBE = 0.044715
+CHUNKS = 2
 
 
 def back_kernel(
@@ -27,7 +28,7 @@
     x_ref, w_ref, g_ref, slope, act_ref, up_ref, q_ref, m_ref, proj,
     gath_a, gath_u, part, from_left, from_right, to_right, to_left, swap_out, swap_in,
     gain_own, gain_in, gain_mid, gain_sum, gain_z,
-    in_sem, sec_send, sec_recv,
+    in_sem, sec_send, sec_recv, u_send, u_recv, s_send, s_recv,
     xy_send, xy_recv, r_send, r_recv, l_send, l_recv, g_send, g_recv,
 ):
     me = lax.axis_index("dp")
@@ -46,6 +47,7 @@
     micro, tok_mb = factor_ref.shape
     step_rows = 16
     width = min(256, channels)
+    part_cols = half // CHUNKS
 
     load_x = pltpu.make_async_copy(x_hbm, x_ref, in_sem.at[0])
     load_w = pltpu.make_async_copy(w_hbm, w_ref, in_sem.at[1])
@@ -107,15 +109,27 @@
 
     act_y = copy(act_ref.at[1 - y], gath_a.at[1], xy_send.at[0], xy_recv.at[0], yn)
     act_x = copy(act_ref.at[y], gath_a.at[0], xy_send.at[1], xy_recv.at[1], xn)
-    up_x = copy(up_ref.at[1 - x], gath_u.at[0], xy_send.at[2], xy_recv.at[2], xn)
-    up_y = copy(up_ref.at[x], gath_u.at[1], xy_send.at[3], xy_recv.at[3], yn)
+    up_x = [
+        copy(up_ref.at[(1 - x) * CHUNKS + k], gath_u.at[k], u_send.at[k], u_recv.at[k], xn)
+        for k in range(CHUNKS)
+    ]
+    up_y = [
+        copy(
+            up_ref.at[x * CHUNKS + k], gath_u.at[CHUNKS + k],
+            u_send.at[CHUNKS + k], u_recv.at[CHUNKS + k], yn,
+        )
+        for k in range(CHUNKS)
+    ]
+    up_d = [
+        copy(
+            gath_u.at[k], gath_u.at[2 * CHUNKS + k],
+            u_send.at[2 * CHUNKS + k], u_recv.at[2 * CHUNKS + k], yn,
+        )
+        for k in range(CHUNKS)
+    ]
     act_d = copy(gath_a.at[1], gath_a.at[2], xy_send.at[4], xy_recv.at[4], xn)
-    up_d = copy(gath_u.at[0], gath_u.at[2], xy_send.at[5], xy_recv.at[5], yn)
     gain_x = copy(gain_own, gain_in.at[0], g_send.at[0], g_recv.at[0], xn)
     gain_y = copy(gain_mid, gain_in.at[1], g_send.at[1], g_recv.at[1], yn)
-    act_y.start()
-    act_x.start()
-
     def relay(mb):
         span = pl.ds(mb * tok_mb, tok_mb)
         return pltpu.make_async_remote_copy(
@@ -126,37 +140,43 @@
 
     @pl.when(sec < last)
     def _():
-        act_y.wait_recv()
-        act_d.start()
+        relay(0).wait_recv()
+
+    act_y.start()
+    act_x.start()
 
     @pl.when(sec == last)
     def _():
         load_g.wait()
 
     for mb in range(micro):
-        @pl.when(sec < last)
-        def _():
-            relay(mb).wait_recv()
+        if mb > 0:
+            @pl.when(sec < last)
+            def _():
+                relay(mb).wait_recv()
 
         @pl.loop(mb * (tok_mb // step_rows), (mb + 1) * (tok_mb // step_rows))
         def _(i):
             r = pl.ds(pl.multiple_of(i * step_rows, step_rows), step_rows)
             m = m_ref[r, :1]
-            for h in range(2):
-                g = g_ref[r, h * half:(h + 1) * half].astype(F32)
+            for h in range(2 * CHUNKS):
+                g = g_ref[r, h * part_cols:(h + 1) * part_cols].astype(F32)
                 up_ref[h, r, :] = (m * g).astype(BF16)
 
-    up_x.start()
-    up_y.start()
+    up_x[0].start()
+    up_y[0].start()
     load_w.wait()
 
     @pl.loop(0, channels // width)
     def _(c):
         cols = pl.ds(pl.multiple_of(c * width, width), width)
         last_dims = (((1,), (1,)), ((), ()))
-        back = lax.dot_general(
-            up_ref[0], w_ref[cols, :half], last_dims, preferred_element_type=F32
-        ) + lax.dot_general(up_ref[1], w_ref[cols, half:], last_dims, preferred_element_type=F32)
+        back = jnp.zeros((tokens, width), F32)
+        for h in range(2 * CHUNKS):
+            back = back + lax.dot_general(
+                up_ref[h], w_ref[cols, h * part_cols:(h + 1) * part_cols], last_dims,
+                preferred_element_type=F32,
+            )
         grad_norm = back * slope[:, cols]
         xc = x_ref[:, cols].astype(F32)
         scaled = grad_norm * gain_ref[:, cols]
@@ -183,36 +203,119 @@
         def _():
             relay(mb).start()
 
-    @pl.when(sec == last)
-    def _():
-        act_y.wait_recv()
-        act_d.start()
-
-    up_x.wait_recv()
-    up_d.start()
+    act_y.wait_recv()
+    act_d.start()
+    up_x[0].wait_recv()
+    up_d[0].start()
     gain_x.start()
-
-    @pl.loop(0, planes)
-    def _(b):
-        cols = pl.ds(pl.multiple_of(b * rows, 128), rows)
-        part[b] = outer_sum(act_ref[y, :, cols], up_ref[x])
-
-    def add_source(slot):
+    for k in range(1, CHUNKS):
+        up_x[k].start()
+        up_y[k].start()
+
+    for k in range(CHUNKS):
         @pl.loop(0, planes)
         def _(b):
             cols = pl.ds(pl.multiple_of(b * rows, 128), rows)
-            part[b] += outer_sum(gath_a[slot, :, cols], gath_u[slot])
+            part[k * planes + b] = outer_sum(act_ref[y, :, cols], up_ref[x * CHUNKS + k])
+
+    def add_source(slot, k):
+        @pl.loop(0, planes)
+        def _(b):
+            cols = pl.ds(pl.multiple_of(b * rows, 128), rows)
+            part[k * planes + b] += outer_sum(gath_a[slot, :, cols], gath_u[slot * CHUNKS + k])
+
+    z_next = lax.rem(me + 4, total)
+    z_prev = lax.rem(me + total - 4, total)
+
+    def right(at):
+        return copy(to_right.at[at], from_left.at[at], r_send.at[at], r_recv.at[at], z_next)
+
+    def left(at):
+        return copy(to_left.at[at], from_right.at[at], l_send.at[at], l_recv.at[at], z_prev)
+
+    def z_step(t, k):
+        @pl.when(t >= z)
+        def _():
+            at = k * planes + planes - 1 - t + z
+
+            @pl.when(z > 0)
+            def _():
+                right(at).wait_recv()
+                to_right[at] = (part[at] + from_left[at].astype(F32)).astype(BF16)
+
+            @pl.when(z == 0)
+            def _():
+                to_right[at] = part[at].astype(BF16)
+
+            right(at).start()
+
+        @pl.when(t >= planes - 1 - z)
+        def _():
+            at = k * planes + t - (planes - 1 - z)
+
+            @pl.when(z < planes - 1)
+            def _():
+                left(at).wait_recv()
+                to_left[at] = (part[at] + from_right[at].astype(F32)).astype(BF16)
+
+            @pl.when(z == planes - 1)
+            def _():
+                to_left[at] = part[at].astype(BF16)
+
+            left(at).start()
 
     act_x.wait_recv()
-    add_source(0)
-    up_y.wait_recv()
-    add_source(1)
+    for k in range(CHUNKS):
+        if k == 0:
+            add_source(0, 0)
+        up_y[k].wait_recv()
+        add_source(1, k)
+        if k == 0:
+            act_d.wait_recv()
+        up_d[k].wait_recv()
+        add_source(2, k)
+        z_step(0, k)
+        if k + 1 < CHUNKS:
+            up_x[k + 1].wait_recv()
+            up_d[k + 1].start()
+        for t in range(1, planes - 1):
+            z_step(t, k)
+        if k + 1 < CHUNKS:
+            add_source(0, k + 1)
+
     gain_x.wait_recv()
     gain_mid[...] = gain_own[...] + gain_in[0]
     gain_y.start()
-    act_d.wait_recv()
-    up_d.wait_recv()
-    add_source(2)
+    other = pl.ds(pl.multiple_of((1 - x) * share, 64), share)
+    own = pl.ds(pl.multiple_of(x * share, 64), share)
+    swaps = [
+        copy(swap_out.at[k], swap_in.at[k], s_send.at[k], s_recv.at[k], xn)
+        for k in range(CHUNKS)
+    ]
+
+    def finish(k):
+        at = k * planes + z
+
+        @pl.when(z > 0)
+        def _():
+            right(at).wait_recv()
+            part[at] += from_left[at].astype(F32)
+
+        @pl.when(z < planes - 1)
+        def _():
+            left(at).wait_recv()
+            part[at] += from_right[at].astype(F32)
+
+        swap_out[k] = part[at, other, :].astype(BF16)
+        swaps[k].start()
+        for side in range(2):
+            @pl.when(x == side)
+            def _():
+                lo = side * half + k * part_cols
+                out_ref[:, lo:lo + part_cols] = part[at, own, :]
+
+    for k in range(CHUNKS - 1):
+        finish(k)
     gain_y.wait_recv()
     gain_sum[...] = gain_mid[...] + gain_in[1]
     gain_zs = [
@@ -222,62 +325,7 @@
     for tiny in gain_zs:
         tiny.start()
 
-    z_next = lax.rem(me + 4, total)
-    z_prev = lax.rem(me + total - 4, total)
-
-    def right(b):
-        return copy(to_right.at[b], from_left.at[b], r_send.at[b], r_recv.at[b], z_next)
-
-    def left(b):
-        return copy(to_left.at[b], from_right.at[b], l_send.at[b], l_recv.at[b], z_prev)
-
-    for t in range(planes - 1):
-        @pl.when(t >= z)
-        def _():
-            b = planes - 1 - t + z
-
-            @pl.when(z > 0)
-            def _():
-                right(b).wait_recv()
-                to_right[b] = (part[b] + from_left[b].astype(F32)).astype(BF16)
-
-            @pl.when(z == 0)
-            def _():
-                to_right[b] = part[b].astype(BF16)
-
-            right(b).start()
-
-        @pl.when(t >= planes - 1 - z)
-        def _():
-            b = t - (planes - 1 - z)
-
-            @pl.when(z < planes - 1)
-            def _():
-                left(b).wait_recv()
-                to_left[b] = (part[b] + from_right[b].astype(F32)).astype(BF16)
-
-            @pl.when(z == planes - 1)
-            def _():
-                to_left[b] = part[b].astype(BF16)
-
-            left(b).start()
-
-    @pl.when(z > 0)
-    def _():
-        right(z).wait_recv()
-        part[z] += from_left[z].astype(F32)
-
-    @pl.when(z < planes - 1)
-    def _():
-        left(z).wait_recv()
-        part[z] += from_right[z].astype(F32)
-
-    other = pl.ds(pl.multiple_of((1 - x) * share, 64), share)
-    own = pl.ds(pl.multiple_of(x * share, 64), share)
-    swap_out[...] = part[z, other, :].astype(BF16)
-    swap = copy(swap_out, swap_in, xy_send.at[6], xy_recv.at[6], xn)
-    swap.start()
-
+    finish(CHUNKS - 1)
     for tiny in gain_zs:
         tiny.wait_recv()
     total_gain = gain_sum[...]
@@ -285,34 +333,25 @@
         total_gain = total_gain + gain_z[step]
     gain_out[...] = total_gain
 
-    @pl.when(x == 0)
-    def _():
-        out_ref[:, :half] = part[z, own, :]
-
-    @pl.when(x == 1)
-    def _():
-        out_ref[:, half:] = part[z, own, :]
-
-    swap.wait_recv()
-
-    @pl.when(x == 0)
-    def _():
-        out_ref[:, half:] = swap_in[...].astype(F32)
-
-    @pl.when(x == 1)
-    def _():
-        out_ref[:, :half] = swap_in[...].astype(F32)
-
-    for sent in [gain_x, act_x, up_y, up_x, act_y, act_d, up_d, gain_y, swap] + gain_zs:
+    for k in range(CHUNKS):
+        swaps[k].wait_recv()
+        for side in range(2):
+            @pl.when(x == side)
+            def _():
+                lo = (1 - side) * half + k * part_cols
+                out_ref[:, lo:lo + part_cols] = swap_in[k].astype(F32)
+
+    for sent in [act_x, act_y, act_d, gain_x, gain_y] + up_x + up_y + up_d + swaps + gain_zs:
         sent.wait_send()
-    for t in range(planes - 1):
-        @pl.when(t >= z)
-        def _():
-            right(planes - 1 - t + z).wait_send()
-
-        @pl.when(t >= planes - 1 - z)
-        def _():
-            left(t - (planes - 1 - z)).wait_send()
+    for k in range(CHUNKS):
+        for t in range(planes - 1):
+            @pl.when(t >= z)
+            def _():
+                right(k * planes + planes - 1 - t + z).wait_send()
+
+            @pl.when(t >= planes - 1 - z)
+            def _():
+                left(k * planes + t - (planes - 1 - z)).wait_send()
 
     @pl.when(sec > 0)
     def _():
@@ -331,8 +370,10 @@
     rows = half // planes
     factor = 1.0 + 0.5 * jnp.sin(2.0 * math.pi * positions.astype(F32) / DEPTH)
     vmem = pl.BlockSpec(memory_space=pltpu.VMEM)
-    hbm = pl.BlockSpec(memory_space=pl.ANY)
-    block = (planes, rows, half)
+    hbm = pl.BlockSpec(memory_space=pltpu.HBM)
+    part_cols = half // CHUNKS
+    hops = CHUNKS * planes
+    block = (hops, rows, part_cols)
     line = (1, channels)
     sems = pltpu.SemaphoreType.DMA
     weight_grad, gain_all, grads = pl.pallas_call(
@@ -350,30 +391,31 @@
             pltpu.VMEM((tokens, channels), BF16),
             pltpu.VMEM((tokens, channels), F32),
             pltpu.VMEM((2, tokens, half), BF16),
-            pltpu.VMEM((2, tokens, half), BF16),
+            pltpu.VMEM((2 * CHUNKS, tokens, part_cols), BF16),
             pltpu.VMEM((tokens, 128), F32),
             pltpu.VMEM((tokens, 128), F32),
             pltpu.VMEM((tokens, 128), F32),
             pltpu.VMEM((3, tokens, half), BF16),
-            pltpu.VMEM((3, tokens, half), BF16),
+            pltpu.VMEM((3 * CHUNKS, tokens, part_cols), BF16),
             pltpu.VMEM(block, F32),
             pltpu.VMEM(block, BF16),
             pltpu.VMEM(block, BF16),
             pltpu.VMEM(block, BF16),
             pltpu.VMEM(block, BF16),
-            pltpu.VMEM((share, half), BF16),
-            pltpu.VMEM((share, half), BF16),
+            pltpu.VMEM((CHUNKS, share, part_cols), BF16),
+            pltpu.VMEM((CHUNKS, share, part_cols), BF16),
             pltpu.VMEM(line, F32),
             pltpu.VMEM((2,) + line, F32),
             pltpu.VMEM(line, F32),
             pltpu.VMEM(line, F32),
             pltpu.VMEM((planes - 1,) + line, F32),
             sems((3,)), sems((micro,)), sems((micro,)),
-            sems((7,)), sems((7,)), sems((planes,)), sems((planes,)),
-            sems((planes,)), sems((planes,)), sems((planes + 1,)), sems((planes + 1,)),
+            sems((3 * CHUNKS,)), sems((3 * CHUNKS,)), sems((CHUNKS,)), sems((CHUNKS,)),
+            sems((5,)), sems((5,)), sems((hops,)), sems((hops,)),
+            sems((hops,)), sems((hops,)), sems((planes + 1,)), sems((planes + 1,)),
         ],
         compiler_params=pltpu.CompilerParams(
-            collective_id=0, has_side_effects=True, vmem_limit_bytes=56 << 20
+            collective_id=0, has_side_effects=True, vmem_limit_bytes=53 << 20
         ),
     )(
         section_inputs.reshape(tokens, channels),

time: 99.7 us -> 88.9 us (0.89)
  Pallas kernels: 91.7 us -> 81.5 us
    pallas_call x1, Pallas kernels: 91.7 us -> 81.5 us  [body(): pl.pallas_call(functools.partial(back_kernel, planes, sections), out_shap...]
    unnamed x2 -> x4, local copies, waits for them, and re-layouts: 4.6 us -> 5.29 us
where the time goes in v3:
time: 88.9 us; the launch traced here: 88.7 us
  Pallas kernels  81.5 us (92%)
  local copies, waits for them, and re-layouts  5.81 us (7%)
    pallas_call x1, Pallas kernels, body(): pl.pallas_call(functools.partial(back_kernel, planes, sections), out_shap...  81.5 us
    unnamed x4, local copies, waits for them, and re-layouts  5.29 us

profile of v3, /device:TPU:0, one launch (start us, length us, event | category | flops | bytes accessed | tf_op | source)
XLA Modules:
  0.0 88.7 jit_solution(7988719906062714740)
XLA Ops:
  0.6 0.7 multiply_add_fusion.factor_ref
  1.4 0.0 copy-start
  1.4 0.7 copy-done
  2.1 81.5 %shard_map.76 = (f32[128,2048]{1,0:T(8,128)}, f32[1,2048]{1,0:T(1,128)S(1)}, bf16[256,2048]{1,0:T(8,128)(2,1)}) custom-call(bf16[256,2048]{1,0:T(8,128)(2,1)} %bitcast.6, bf16[2048,2048]{1,0:T(8,128)(2,1)} %bitcast.5, bf16[256,2048]{1,0:T(8,128)(2,1)} %bitcast.7, f32[1,2048]{1,0:T(1,128)S(1)} %copy-done, f32[2,128]{1,0:T(2,128)S(1)} %multiply_add_fusion.factor_ref), custom_call_target="tpu_custom_call" | custom-call | tf_op jit(solution)/shard_map/pallas_call | solution.py:379
  83.6 0.5 constant_dynamic-slice_fusion
  84.1 2.3 %copy.10 = bf16[1,2,128,2048]{3,2,1,0:T(8,128)(2,1)} copy(bf16[1,2,128,2048]{3,2,1,0:T(8,128)(2,1)} %bitcast.9) | data formatting | bytes 2097152
  86.4 2.3 %copy.11 = f32[1,128,2048]{2,1,0:T(8,128)} copy(f32[1,128,2048]{2,1,0:T(8,128)} %bitcast.8) | data formatting | bytes 2097152
Async XLA Ops:
  1.4 0.7 copy-start

commit v4 on v3

--- a/solution.py
+++ b/solution.py
@@ -415,7 +415,7 @@
             sems((hops,)), sems((hops,)), sems((planes + 1,)), sems((planes + 1,)),
         ],
         compiler_params=pltpu.CompilerParams(
-            collective_id=0, has_side_effects=True, vmem_limit_bytes=53 << 20
+            collective_id=0, has_side_effects=True, vmem_limit_bytes=50 << 20
         ),
     )(
         section_inputs.reshape(tokens, channels),

time: 88.9 us -> 85.1 us (0.957)
  Pallas kernels: 81.5 us -> 79.1 us
  local copies, waits for them, and re-layouts: 5.81 us -> 4.38 us
    pallas_call x1, Pallas kernels: 81.5 us -> 79.1 us  [body(): pl.pallas_call(functools.partial(back_kernel, planes, sections), out_shap...]
    unnamed x4 -> x6, local copies, waits for them, and re-layouts: 5.29 us -> 3.86 us
where the time goes in v4:
time: 85.1 us; the launch traced here: 84.9 us
  Pallas kernels  79.1 us (93%)
  local copies, waits for them, and re-layouts  4.38 us (5%)
    pallas_call x1, Pallas kernels, body(): pl.pallas_call(functools.partial(back_kernel, planes, sections), out_shap...  79.1 us
    unnamed x6, local copies, waits for them, and re-layouts  3.86 us

profile of v4, /device:TPU:0, one launch (start us, length us, event | category | flops | bytes accessed | tf_op | source)
XLA Modules:
  0.0 84.9 jit_solution(10039249831344254470)
XLA Ops:
  0.6 0.7 multiply_add_fusion.factor_ref
  1.4 0.0 copy-start
  1.4 1.2 %copy-done = bf16[1,2,128,2048]{3,2,1,0:T(8,128)(2,1)S(1)} copy-done((bf16[1,2,128,2048]{3,2,1,0:T(8,128)(2,1)S(1)}, bf16[1,2,128,2048]{3,2,1,0:T(8,128)(2,1)}, u32[]{:S(2)}) %copy-start) | copy-done | bytes 1048600
  2.6 0.0 copy-start.1
  2.6 0.7 copy-done.1
  3.3 79.1 %shard_map.76 = (f32[128,2048]{1,0:T(8,128)S(1)}, f32[1,2048]{1,0:T(1,128)S(1)}, bf16[256,2048]{1,0:T(8,128)(2,1)S(1)}) custom-call(bf16[256,2048]{1,0:T(8,128)(2,1)S(1)} %bitcast.5, bf16[2048,2048]{1,0:T(8,128)(2,1)} %bitcast.8, bf16[256,2048]{1,0:T(8,128)(2,1)} %bitcast.9, f32[1,2048]{1,0:T(1,128)S(1)} %copy-done.1, f32[2,128]{1,0:T(2,128)S(1)} %multiply_add_fusion.factor_ref), custom_call_target="tpu_custom_call" | custom-call | tf_op jit(solution)/shard_map/pallas_call | solution.py:379
  82.4 0.5 constant_dynamic-slice_fusion
  83.0 1.0 %copy.10 = bf16[1,2,128,2048]{3,2,1,0:T(8,128)(2,1)} copy(bf16[1,2,128,2048]{3,2,1,0:T(8,128)(2,1)S(1)} %bitcast.7) | data formatting | bytes 2097152
  83.9 1.0 %copy.11 = f32[1,128,2048]{2,1,0:T(8,128)} copy(f32[1,128,2048]{2,1,0:T(8,128)S(1)} %bitcast.6) | data formatting | bytes 2097152
Async XLA Ops:
  1.4 1.2 %copy-start = (bf16[1,2,128,2048]{3,2,1,0:T(8,128)(2,1)S(1)}, bf16[1,2,128,2048]{3,2,1,0:T(8,128)(2,1)}, u32[]{:S(2)}) copy-start(bf16[1,2,128,2048]{3,2,1,0:T(8,128)(2,1)} %param.5) | copy-start | bytes 3145732
  2.6 0.7 copy-start.1
